TPU v7x, 32 devices: a whole 2x2x4 slice. The times are simulated.
32 devices in a mesh: group: 4 (over y, core), tile: 8 (over z, x).
Axes of the slice: x: 2, y: 2, z: 4, core: 2. Of those that a mesh axis runs over, the one named last changes fastest.
Arguments:
- checkpoint: float32 [16, 512, 768], P(None, ('group', 'tile')), may hold values from -6 to 6
- adjoint_in: float32 [16, 512, 768], P(None, ('group', 'tile')), may hold values from -6 to 6
- courant_x: float32 [16, 512, 768], P(None, ('group', 'tile')), may hold values from 0.05 to 0.5
- courant_y: float32 [16, 512, 768], P(None, ('group', 'tile')), may hold values from 0.05 to 0.5
- mixing: float32 [15, 512, 768], P(None, ('group', 'tile')), may hold values from 0.02 to 0.3
- snd_column: int32 [32, 8, 128], P(('group', 'tile')), may hold values from 0 to 12287
- snd_count: int32 [32, 8], P(('group', 'tile')), may hold values from 32 to 128, as said below
- snd_step: int32 [32, 8, 128], P(('group', 'tile')), may hold values from 0 to 1
- snd_value: float32 [32, 8, 128], P(('group', 'tile')), may hold values from -6 to 6
- snd_weight: float32 [32, 8, 128], P(('group', 'tile')), may hold values from 0.3 to 3
- snd_kernel: float32 [32, 8, 16, 128], P(('group', 'tile')), may hold values from 0 to 0.5
Outputs:
- adjoint_out: float32 [16, 512, 768], P(None, ('group', 'tile'))
Inputs may be any that keep to these rules, and one draw needn't show every extreme that they name: `snd_count`: at most 128; in every draw some destination tile receives 128 soundings from every source device of each group, and every source device fills all slots of some destination tile.
All inputs are finite; a program needn't handle non-finite values.
Results may differ from a plain program's by a relative error of at most 0.0001.
Values sent between devices are 32-bit elements; how exact they have to be, the bound alone decides.
A program may use at most 64 MiB of HBM per device.

v0:
```python
import jax
import jax.numpy as jnp
from jax import lax
from jax.sharding import PartitionSpec as P

STEPS = 2


def with_halo(block, sides, width):
    for axis, dim in sides:
        count = lax.axis_size(axis)
        forward = [(i, i + 1) for i in range(count - 1)]
        forward.append((count - 1, 0))
        backward = [(target, source) for source, target in forward]
        low = lax.ppermute(
            lax.slice_in_dim(block, block.shape[dim] - width, None, axis=dim), axis, forward
        )
        high = lax.ppermute(lax.slice_in_dim(block, 0, width, axis=dim), axis, backward)
        block = jnp.concatenate([low, block, high], axis=dim)
    return block


def from_behind(block, axis, distance):
    devices = range(lax.axis_size(axis))
    route = [((i - distance) % len(devices), i) for i in devices]
    return lax.ppermute(block, axis, route)


def pad_periodic(field, width, along):
    total = field.shape[along]
    return jnp.concatenate(
        [
            lax.slice_in_dim(field, total - width, total, axis=along),
            field,
            lax.slice_in_dim(field, 0, width, axis=along),
        ],
        axis=along,
    )


def sweep_forward(padded, courant_pad, along):
    interior = padded.shape[along] - 4

    def piece_of(first, last):
        return lax.slice_in_dim(padded, first, last, axis=along)

    courant_face = lax.slice_in_dim(courant_pad, 0, interior + 1, axis=along)
    fluxes = (
        courant_face
        * (
            2.0 * piece_of(2, interior + 3)
            + 5.0 * piece_of(1, interior + 2)
            - piece_of(0, interior + 1)
        )
        / 6.0
    )
    return (
        piece_of(2, interior + 2)
        + lax.slice_in_dim(fluxes, 0, interior, axis=along)
        - lax.slice_in_dim(fluxes, 1, interior + 1, axis=along)
    )


def sweep_adjoint(padded, courant_pad, along):
    interior = padded.shape[along] - 4

    def piece_of(first, last):
        return lax.slice_in_dim(padded, first, last, axis=along)

    differences = piece_of(2, interior + 4) - piece_of(1, interior + 3)
    scaled = courant_pad * differences
    return (
        piece_of(2, interior + 2)
        + (
            2.0 * lax.slice_in_dim(scaled, 0, interior, axis=along)
            + 5.0 * lax.slice_in_dim(scaled, 1, interior + 1, axis=along)
            - lax.slice_in_dim(scaled, 2, interior + 2, axis=along)
        )
        / 6.0
    )


def vertical_mix(field, mixing):
    fluxes = mixing * (field[1:] - field[:-1])
    zero_row = jnp.zeros_like(field[:1])
    return (
        field
        + jnp.concatenate([fluxes, zero_row], axis=0)
        - jnp.concatenate([zero_row, fluxes], axis=0)
    )


def horizontal(rimmed, wind_x, wind_y):
    swept = sweep_forward(rimmed, wind_x, 1)
    return sweep_forward(pad_periodic(swept, 2, 2), wind_y, 2)


def on_device(
    checkpoint,
    adjoint_in,
    courant_x,
    courant_y,
    mixing,
    snd_column,
    snd_count,
    snd_step,
    snd_value,
    snd_weight,
    snd_kernel,
):
    levels, width_x, width_y = checkpoint.shape
    tile_count = snd_column.shape[1]
    capacity = snd_column.shape[2]
    wind_x = with_halo(courant_x, ((("group", "tile"), 1),), 1)
    wind_y = pad_periodic(courant_y, 1, 2)
    tracer = from_behind(checkpoint, "group", 1)
    rimmed = with_halo(tracer, ((("group", "tile"), 1),), 2)
    tracer = vertical_mix(horizontal(rimmed, wind_x, wind_y), mixing)
    states = [tracer]
    moment = 1
    rimmed = with_halo(tracer, ((("group", "tile"), 1),), 2)
    tracer = vertical_mix(horizontal(rimmed, wind_x, wind_y), mixing)
    states.append(tracer)
    position = lax.broadcasted_iota(jnp.int32, snd_column.shape, 2)
    weight = jnp.where(position < snd_count[:, :, None], snd_weight, jnp.zeros_like(snd_weight))
    values, weights, kernels = (
        lax.all_to_all(snd_value, "tile", split_axis=1, concat_axis=0, tiled=True),
        lax.all_to_all(weight, "tile", split_axis=1, concat_axis=0, tiled=True),
        lax.all_to_all(snd_kernel, "tile", split_axis=1, concat_axis=0, tiled=True),
    )
    columns, step_ids = (
        lax.all_to_all(snd_column, "tile", split_axis=1, concat_axis=0, tiled=True),
        lax.all_to_all(snd_step, "tile", split_axis=1, concat_axis=0, tiled=True),
    )
    values = values.reshape(tile_count, capacity)
    weights = weights.reshape(tile_count, capacity)
    kernels = kernels.reshape(tile_count, levels, capacity)
    step_ids = step_ids.reshape(tile_count, capacity)
    cell_index = columns.reshape(-1)
    forcings = []
    for moment in range(STEPS):
        flattened = states[moment].reshape(levels, -1)
        picked = jnp.take(flattened, cell_index, axis=1).reshape(levels, tile_count, capacity)
        observed = jnp.einsum("ltc,tlc->tc", picked, kernels, precision=lax.Precision.HIGHEST)
        misfit = jnp.where(
            step_ids == moment, weights * (observed - values), jnp.zeros_like(observed)
        )
        contribution = jnp.einsum(
            "tlc,tc->ltc", kernels, misfit, precision=lax.Precision.HIGHEST
        ).reshape(levels, -1)
        forcing = (
            jnp.zeros((levels, width_x * width_y), jnp.float32).at[:, cell_index].add(contribution)
        )
        forcings.append(forcing.reshape(levels, width_x, width_y))
    adjoint = adjoint_in
    for moment in reversed(range(STEPS)):
        adjoint = vertical_mix(adjoint + forcings[moment], mixing)
        adjoint = sweep_adjoint(pad_periodic(adjoint, 2, 2), wind_y, 2)
        rimmed = with_halo(adjoint, ((("group", "tile"), 1),), 2)
        adjoint = sweep_adjoint(rimmed, wind_x, 1)
    return adjoint


def solution(mesh):
    return jax.shard_map(
        on_device,
        mesh=mesh,
        in_specs=(
            P(None, ("group", "tile"), None),
            P(None, ("group", "tile"), None),
            P(None, ("group", "tile"), None),
            P(None, ("group", "tile"), None),
            P(None, ("group", "tile"), None),
            P(("group", "tile"), None, None),
            P(("group", "tile"), None),
            P(("group", "tile"), None, None),
            P(("group", "tile"), None, None),
            P(("group", "tile"), None, None),
            P(("group", "tile"), None, None, None),
        ),
        out_specs=P(None, ("group", "tile"), None),
        check_vma=False,
    )
```

profile of v0, /device:TPU:0, one launch (start us, length us, event | category | flops | bytes accessed | tf_op | source)
XLA Modules:
  0.0 144.3 jit_solution(1064985473383274465)
XLA Ops:
  0.0 7.4 %all-to-all-start = ((s32[1,8,128]{2,0,1:T(1,128)}), s32[1,8,128]{2,0,1:T(1,128)S(1)}, u32[]{:S(2)}, u32[]{:S(2)}) async-start(s32[1,8,128]{2,0,1:T(1,128)} %bitcast.75), calls=%async_computation | async-start | bytes 8192 | tf_op jit(solution)/shard_map/all_to_all | solution.py:132
  13.8 5.0 %all-to-all-start.2 = ((f32[1,8,128]{2,0,1:T(1,128)}), f32[1,8,128]{2,0,1:T(1,128)S(1)}, u32[]{:S(2)}, u32[]{:S(2)}) async-start(f32[1,8,128]{2,0,1:T(1,128)} %compare_select_fusion.1), calls=%async_computation.2 | async-start | bytes 8192 | tf_op jit(solution)/shard_map/all_to_all | solution.py:128
  21.2 3.8 %collective-permute-start.2 = (f32[16,2,768]{2,1,0:T(2,128)S(1)}, f32[16,2,768]{2,1,0:T(2,128)S(1)}, u32[]{:S(2)}, u32[]{:S(2)}) collective-permute-start(f32[16,2,768]{2,1,0:T(2,128)S(1)} %get-tuple-element.26), channel_id=1, source_target_pairs={{1,0},{2,1},{3,2},{4,3},{5,4},{6,5},{7,6},{8,7},{9,8},{10,9},{11,1... | collective-permute-start | bytes 294920 | tf_op jit(solution)/shard_map/ppermute | solution.py:18
  25.1 3.3 %collective-permute-done.3 = f32[16,2,768]{2,1,0:T(2,128)S(1)} collective-permute-done((f32[16,2,768]{2,1,0:T(2,128)S(1)}, f32[16,2,768]{2,1,0:T(2,128)S(1)}, u32[]{:S(2)}, u32[]{:S(2)}) %collective-permute-start.3) | collective-permute-done | bytes 98336 | tf_op jit(solution)/shard_map/ppermute | solution.py:15
  33.0 5.3 %collective-permute-start.4 = (f32[16,2,768]{2,1,0:T(2,128)}, f32[16,2,768]{2,1,0:T(2,128)}, u32[]{:S(2)}, u32[]{:S(2)}) collective-permute-start(f32[16,2,768]{2,1,0:T(2,128)} %get-tuple-element.22), channel_id=1, source_target_pairs={{1,0},{2,1},{3,2},{4,3},{5,4},{6,5},{7,6},{8,7},{9,8},{10,9},{11,1... | collective-permute-start | bytes 294920 | tf_op jit(solution)/shard_map/ppermute | solution.py:18
  38.3 3.9 %copy.49 = f32[16,16,768]{0,2,1:T(8,128)} copy(f32[16,16,768]{2,1,0:T(8,128)S(1)} %pad_subtract_fusion.3) | data formatting | bytes 1572864 | tf_op jit(solution)/shard_map/sub | solution.py:87
  42.3 6.8 %gather_fusion.1 = f32[1024,16]{1,0:T(8,128)} fusion(f32[16,12288]{0,1:T(8,128)} %bitcast.66, s32[1024]{0:T(1024)S(1)} %fusion.53), kind=kCustom, calls=%fused_computation.1.clone | custom fusion | bytes 135168 | tf_op jit(solution)/shard_map/jit(_take)/gather | solution.py:143
  52.9 3.3 %all-to-all-start.4 = ((f32[1,8,128]{2,0,1:T(1,128)}), f32[1,8,128]{2,0,1:T(1,128)S(1)}, u32[]{:S(2)}, u32[]{:S(2)}) async-start(f32[1,8,128]{2,0,1:T(1,128)} %bitcast.22), calls=%async_computation.4 | async-start | bytes 8192 | tf_op jit(solution)/shard_map/all_to_all | solution.py:127
  56.3 2.3 %pad_subtract_fusion.2 = f32[16,16,768]{2,1,0:T(8,128)} fusion(f32[15,16,768]{2,1,0:T(8,128)} %fusion.47, f32[16,16,768]{2,1,0:T(8,128)S(1)} %slice_subtract_fusion.4), kind=kLoop, calls=%fused_computation.95 | loop fusion | flops 393216 | bytes 2310144 | tf_op jit(solution)/shard_map/sub | solution.py:87
  58.6 4.8 %copy.42 = f32[16,16,768]{0,2,1:T(8,128)} copy(f32[16,16,768]{2,1,0:T(8,128)} %pad_subtract_fusion.2) | data formatting | bytes 1572864 | tf_op jit(solution)/shard_map/sub | solution.py:87
  63.5 6.8 %gather_fusion = f32[1024,16]{1,0:T(8,128)} fusion(f32[16,12288]{0,1:T(8,128)} %bitcast.65, s32[1024]{0:T(1024)S(1)} %fusion.53), kind=kCustom, calls=%fused_computation.clone | custom fusion | bytes 135168 | tf_op jit(solution)/shard_map/jit(_take)/gather | solution.py:143
  70.3 5.9 %all-to-all-start.3 = ((f32[1,8,16,128]{3,2,0,1:T(8,128)}), f32[1,8,16,128]{3,2,0,1:T(8,128)S(1)}, u32[]{:S(2)}, u32[]{:S(2)}) async-start(f32[1,8,16,128]{3,2,0,1:T(8,128)} %bitcast.19), calls=%async_computation.3 | async-start | bytes 131072 | tf_op jit(solution)/shard_map/all_to_all | solution.py:129
  76.2 2.2 %broadcast_select_fusion = (f32[1024,16]{1,0:T(8,128)S(1)}, f32[1024,16]{1,0:T(8,128)}) fusion(f32[1024,16]{1,0:T(8,128)} %gather_fusion.1, pred[1024]{0:T(1024)(128)(4,1)S(1)} %compare_and_fusion, f32[1024,16]{1,0:T(8,128)} %gather_fusion), kind=kLoop, calls=%fused_computation.105 | loop fusion | flops 32768 | bytes 263168 | tf_op jit(solution)/shard_map/jit(_take)/select_n | solution.py:143
  79.8 3.3 %all-to-all-done.3 = f32[1,8,16,128]{3,2,0,1:T(8,128)S(1)} async-done(((f32[1,8,16,128]{3,2,0,1:T(8,128)}), f32[1,8,16,128]{3,2,0,1:T(8,128)S(1)}, u32[]{:S(2)}, u32[]{:S(2)}) %all-to-all-start.3) | async-done | bytes 65568 | tf_op jit(solution)/shard_map/all_to_all | solution.py:129
  83.1 3.3 %all-to-all-start.1 = ((s32[1,8,128]{2,0,1:T(1,128)}), s32[1,8,128]{2,0,1:T(1,128)S(1)}, u32[]{:S(2)}, u32[]{:S(2)}) async-start(s32[1,8,128]{2,0,1:T(1,128)} %bitcast.7), calls=%async_computation.1 | async-start | bytes 8192 | tf_op jit(solution)/shard_map/all_to_all | solution.py:133
  86.5 6.3 %all-to-all-done.1 = s32[1,8,128]{2,0,1:T(1,128)S(1)} async-done(((s32[1,8,128]{2,0,1:T(1,128)}), s32[1,8,128]{2,0,1:T(1,128)S(1)}, u32[]{:S(2)}, u32[]{:S(2)}) %all-to-all-start.1) | async-done | bytes 4128 | tf_op jit(solution)/shard_map/all_to_all | solution.py:133
  93.0 9.0 %scatter_custom_fusion = f32[16,12288]{0,1:T(8,128)} fusion(s32[1024]{0:T(1024)S(1)} %bitcast.76, f32[1024,16]{1,0:T(8,128)S(1)} %copy.46, f32[]{:T(128)} %constant.15.clone.1), kind=kCustom, calls=%fused_computation.6 | custom fusion | flops 16384 | bytes 786436 | tf_op jit(solution)/shard_map/scatter-add | solution.py:152
  102.1 4.5 %copy.47 = f32[16,16,768]{2,1,0:T(8,128)S(1)} copy(f32[16,16,768]{0,2,1:T(8,128)} %bitcast.64) | data formatting | bytes 1572864 | tf_op jit(solution)/shard_map/reshape | solution.py:154
  109.9 2.0 %collective-permute-start.8 = (f32[16,2,768]{2,1,0:T(2,128)}, f32[16,2,768]{2,1,0:T(2,128)}, u32[]{:S(2)}, u32[]{:S(2)}) collective-permute-start(f32[16,2,768]{2,1,0:T(2,128)} %get-tuple-element.14), channel_id=1, source_target_pairs={{0,1},{1,2},{2,3},{3,4},{4,5},{5,6},{6,7},{7,8},{8,9},{9,10},{10,1... | collective-permute-start | bytes 294920 | tf_op jit(solution)/shard_map/ppermute | solution.py:15
  111.9 3.3 %collective-permute-start.6 = (f32[16,1,768]{2,1,0:T(1,128)}, f32[16,1,768]{2,1,0:T(1,128)S(1)}, u32[]{:S(2)}, u32[]{:S(2)}) collective-permute-start(f32[16,1,768]{2,1,0:T(1,128)} %get-tuple-element.12), channel_id=1, source_target_pairs={{1,0},{2,1},{3,2},{4,3},{5,4},{6,5},{7,6},{8,7},{9,8},{10,9},{11,1... | collective-permute-start | bytes 147464 | tf_op jit(solution)/shard_map/ppermute | solution.py:18
  116.3 9.4 %scatter_custom_fusion.1 = f32[16,12288]{0,1:T(8,128)} fusion(s32[1024]{0:T(1024)S(1)} %bitcast.77, f32[1024,16]{1,0:T(8,128)} %copy.51, f32[]{:T(128)} %constant.15.clone.1), kind=kCustom, calls=%fused_computation.4 | custom fusion | flops 16384 | bytes 786944 | tf_op jit(solution)/shard_map/scatter-add | solution.py:152
  125.7 5.3 %copy.52 = f32[16,16,768]{2,1,0:T(8,128)} copy(f32[16,16,768]{0,2,1:T(8,128)} %bitcast.63) | data formatting | bytes 1572864 | tf_op jit(solution)/shard_map/reshape | solution.py:154
  136.4 2.6 %collective-permute-done.9 = f32[16,2,768]{2,1,0:T(2,128)S(1)} collective-permute-done((f32[16,2,768]{2,1,0:T(2,128)S(1)}, f32[16,2,768]{2,1,0:T(2,128)S(1)}, u32[]{:S(2)}, u32[]{:S(2)}) %collective-permute-start.9) | collective-permute-done | bytes 98336 | tf_op jit(solution)/shard_map/ppermute | solution.py:18
  139.0 3.7 %collective-permute-done.10 = f32[16,2,768]{2,1,0:T(2,128)S(1)} collective-permute-done((f32[16,2,768]{2,1,0:T(2,128)S(1)}, f32[16,2,768]{2,1,0:T(2,128)S(1)}, u32[]{:S(2)}, u32[]{:S(2)}) %collective-permute-start.10) | collective-permute-done | bytes 98336 | tf_op jit(solution)/shard_map/ppermute | solution.py:15
  (72 shorter events, 30.0 us)
Async XLA Ops:
  0.0 28.4 %copy-start.1 = (f32[16,16,768]{2,1,0:T(8,128)S(1)}, f32[16,16,768]{2,1,0:T(8,128)}, u32[]{:S(2)}) copy-start(f32[16,16,768]{2,1,0:T(8,128)} %param.15) | copy-start | bytes 2359300
  0.0 13.8 %all-to-all-start = ((s32[1,8,128]{2,0,1:T(1,128)}), s32[1,8,128]{2,0,1:T(1,128)S(1)}, u32[]{:S(2)}, u32[]{:S(2)}) async-start(s32[1,8,128]{2,0,1:T(1,128)} %bitcast.75), calls=%async_computation | async-start | bytes 8192 | tf_op jit(solution)/shard_map/all_to_all | solution.py:132
  7.4 12.2 %collective-permute-start = (f32[16,16,768]{2,1,0:T(8,128)}, f32[16,16,768]{2,1,0:T(8,128)S(1)}, u32[]{:S(2)}, u32[]{:S(2)}) collective-permute-start(f32[16,16,768]{2,1,0:T(8,128)} %param.13), channel_id=1, source_target_pairs={{24,0},{0,8},{8,16},{16,24},{25,1},{1,9},{9,17},{17,25},{26,2},{2,... | collective-permute-start | bytes 2359304 | tf_op jit(solution)/shard_map/ppermute | solution.py:26
  9.2 15.8 %collective-permute-start.1 = (f32[16,1,768]{2,1,0:T(1,128)S(1)}, f32[16,1,768]{2,1,0:T(1,128)S(1)}, u32[]{:S(2)}, u32[]{:S(2)}) collective-permute-start(f32[16,1,768]{2,1,0:T(1,128)S(1)} %get-tuple-element.13), channel_id=1, source_target_pairs={{0,1},{1,2},{2,3},{3,4},{4,5},{5,6},{6,7},{7,8},{8,9},{9,10},{10,1... | collective-permute-start | bytes 147464 | tf_op jit(solution)/shard_map/ppermute | solution.py:15
  13.8 39.1 %all-to-all-start.2 = ((f32[1,8,128]{2,0,1:T(1,128)}), f32[1,8,128]{2,0,1:T(1,128)S(1)}, u32[]{:S(2)}, u32[]{:S(2)}) async-start(f32[1,8,128]{2,0,1:T(1,128)} %compare_select_fusion.1), calls=%async_computation.2 | async-start | bytes 8192 | tf_op jit(solution)/shard_map/all_to_all | solution.py:128
  19.6 8.7 %collective-permute-start.3 = (f32[16,2,768]{2,1,0:T(2,128)S(1)}, f32[16,2,768]{2,1,0:T(2,128)S(1)}, u32[]{:S(2)}, u32[]{:S(2)}) collective-permute-start(f32[16,2,768]{2,1,0:T(2,128)S(1)} %get-tuple-element.27), channel_id=1, source_target_pairs={{0,1},{1,2},{2,3},{3,4},{4,5},{5,6},{6,7},{7,8},{8,9},{9,10},{10,1... | collective-permute-start | bytes 294920 | tf_op jit(solution)/shard_map/ppermute | solution.py:15
  21.2 7.2 %collective-permute-start.2 = (f32[16,2,768]{2,1,0:T(2,128)S(1)}, f32[16,2,768]{2,1,0:T(2,128)S(1)}, u32[]{:S(2)}, u32[]{:S(2)}) collective-permute-start(f32[16,2,768]{2,1,0:T(2,128)S(1)} %get-tuple-element.26), channel_id=1, source_target_pairs={{1,0},{2,1},{3,2},{4,3},{5,4},{6,5},{7,6},{8,7},{9,8},{10,9},{11,1... | collective-permute-start | bytes 294920 | tf_op jit(solution)/shard_map/ppermute | solution.py:18
  29.0 1.1 copy-start
  30.9 1.1 copy-start.2
  33.0 16.1 %collective-permute-start.5 = (f32[16,2,768]{2,1,0:T(2,128)}, f32[16,2,768]{2,1,0:T(2,128)S(1)}, u32[]{:S(2)}, u32[]{:S(2)}) collective-permute-start(f32[16,2,768]{2,1,0:T(2,128)} %get-tuple-element.23), channel_id=1, source_target_pairs={{0,1},{1,2},{2,3},{3,4},{4,5},{5,6},{6,7},{7,8},{8,9},{9,10},{10,1... | collective-permute-start | bytes 294920 | tf_op jit(solution)/shard_map/ppermute | solution.py:15
  33.0 16.1 %collective-permute-start.4 = (f32[16,2,768]{2,1,0:T(2,128)}, f32[16,2,768]{2,1,0:T(2,128)}, u32[]{:S(2)}, u32[]{:S(2)}) collective-permute-start(f32[16,2,768]{2,1,0:T(2,128)} %get-tuple-element.22), channel_id=1, source_target_pairs={{1,0},{2,1},{3,2},{4,3},{5,4},{6,5},{7,6},{8,7},{9,8},{10,9},{11,1... | collective-permute-start | bytes 294920 | tf_op jit(solution)/shard_map/ppermute | solution.py:18
  52.9 17.3 %all-to-all-start.4 = ((f32[1,8,128]{2,0,1:T(1,128)}), f32[1,8,128]{2,0,1:T(1,128)S(1)}, u32[]{:S(2)}, u32[]{:S(2)}) async-start(f32[1,8,128]{2,0,1:T(1,128)} %bitcast.22), calls=%async_computation.4 | async-start | bytes 8192 | tf_op jit(solution)/shard_map/all_to_all | solution.py:127
  70.3 12.8 %all-to-all-start.3 = ((f32[1,8,16,128]{3,2,0,1:T(8,128)}), f32[1,8,16,128]{3,2,0,1:T(8,128)S(1)}, u32[]{:S(2)}, u32[]{:S(2)}) async-start(f32[1,8,16,128]{3,2,0,1:T(8,128)} %bitcast.19), calls=%async_computation.3 | async-start | bytes 131072 | tf_op jit(solution)/shard_map/all_to_all | solution.py:129
  83.1 9.7 %all-to-all-start.1 = ((s32[1,8,128]{2,0,1:T(1,128)}), s32[1,8,128]{2,0,1:T(1,128)S(1)}, u32[]{:S(2)}, u32[]{:S(2)}) async-start(s32[1,8,128]{2,0,1:T(1,128)} %bitcast.7), calls=%async_computation.1 | async-start | bytes 8192 | tf_op jit(solution)/shard_map/all_to_all | solution.py:133
  109.9 21.1 %collective-permute-start.7 = (f32[16,2,768]{2,1,0:T(2,128)}, f32[16,2,768]{2,1,0:T(2,128)}, u32[]{:S(2)}, u32[]{:S(2)}) collective-permute-start(f32[16,2,768]{2,1,0:T(2,128)} %get-tuple-element.15), channel_id=1, source_target_pairs={{1,0},{2,1},{3,2},{4,3},{5,4},{6,5},{7,6},{8,7},{9,8},{10,9},{11,1... | collective-permute-start | bytes 294920 | tf_op jit(solution)/shard_map/ppermute | solution.py:18
  109.9 21.1 %collective-permute-start.8 = (f32[16,2,768]{2,1,0:T(2,128)}, f32[16,2,768]{2,1,0:T(2,128)}, u32[]{:S(2)}, u32[]{:S(2)}) collective-permute-start(f32[16,2,768]{2,1,0:T(2,128)} %get-tuple-element.14), channel_id=1, source_target_pairs={{0,1},{1,2},{2,3},{3,4},{4,5},{5,6},{6,7},{7,8},{8,9},{9,10},{10,1... | collective-permute-start | bytes 294920 | tf_op jit(solution)/shard_map/ppermute | solution.py:15
  111.9 19.1 %collective-permute-start.6 = (f32[16,1,768]{2,1,0:T(1,128)}, f32[16,1,768]{2,1,0:T(1,128)S(1)}, u32[]{:S(2)}, u32[]{:S(2)}) collective-permute-start(f32[16,1,768]{2,1,0:T(1,128)} %get-tuple-element.12), channel_id=1, source_target_pairs={{1,0},{2,1},{3,2},{4,3},{5,4},{6,5},{7,6},{8,7},{9,8},{10,9},{11,1... | collective-permute-start | bytes 147464 | tf_op jit(solution)/shard_map/ppermute | solution.py:18
  131.0 1.5 %copy-start.3 = (f32[16,16,768]{2,1,0:T(8,128)S(1)}, f32[16,16,768]{2,1,0:T(8,128)}, u32[]{:S(2)}) copy-start(f32[16,16,768]{2,1,0:T(8,128)} %copy.52) | copy-start | bytes 2359300
  134.3 4.7 %collective-permute-start.9 = (f32[16,2,768]{2,1,0:T(2,128)S(1)}, f32[16,2,768]{2,1,0:T(2,128)S(1)}, u32[]{:S(2)}, u32[]{:S(2)}) collective-permute-start(f32[16,2,768]{2,1,0:T(2,128)S(1)} %get-tuple-element.9), channel_id=1, source_target_pairs={{1,0},{2,1},{3,2},{4,3},{5,4},{6,5},{7,6},{8,7},{9,8},{10,9},{11,1... | collective-permute-start | bytes 294920 | tf_op jit(solution)/shard_map/ppermute | solution.py:18
  134.4 8.3 %collective-permute-start.10 = (f32[16,2,768]{2,1,0:T(2,128)S(1)}, f32[16,2,768]{2,1,0:T(2,128)S(1)}, u32[]{:S(2)}, u32[]{:S(2)}) collective-permute-start(f32[16,2,768]{2,1,0:T(2,128)S(1)} %get-tuple-element.8), channel_id=1, source_target_pairs={{0,1},{1,2},{2,3},{3,4},{4,5},{5,6},{6,7},{7,8},{8,9},{9,10},{10,1... | collective-permute-start | bytes 294920 | tf_op jit(solution)/shard_map/ppermute | solution.py:15
where the time goes:
time: 145 us; the launch traced here: 144 us
  starting transfers between devices  45.2 us (31%)
  local copies, waits for them, and re-layouts  41.3 us (28%)
  other arithmetic  37.4 us (26%)
  waiting for transfers between devices  20.1 us (14%)
    scatter-add x2, other arithmetic, on_device(): jnp.zeros((levels, width_x * width_y), jnp.float32).at[:, cell_index]  18.4 us
    gather x2, local copies, waits for them, and re-layouts, on_device(): jnp.take(flattened, cell_index, axis=1)  13.6 us
    ppermute x5, starting transfers between devices, with_halo(): lax.ppermute(lax.slice_in_dim(block, 0, width, axis=dim), axis, backward)  12.6 us
    reshape x2, local copies, waits for them, and re-layouts, on_device(): forcings.append(forcing.reshape(levels, width_x, width_y))  9.79 us
    sub x2, local copies, waits for them, and re-layouts, vertical_mix(): field + jnp.concatenate([fluxes, zero_row], axis=0)  8.8 us
    ppermute x5, starting transfers between devices, with_halo(): lax.ppermute(lax.slice_in_dim(block, block.shape[dim] - width, None, axis...  7.6 us
    all_to_all x1, starting transfers between devices, on_device(): lax.all_to_all(snd_column, 'tile', split_axis=1, concat_axis=0, tiled=True)  7.41 us
    ppermute x5, waiting for transfers between devices, with_halo(): lax.ppermute(lax.slice_in_dim(block, block.shape[dim] - width, None, axis...  7 us
  transfers between devices with their start and end apart: 16, of which 7 were waited for; matrix products, arithmetic and copies ran while one was open for 38% of the time, Pallas kernels for 0%

commit v1 on v0

v1 whole, which is shorter than its diff:
```python
import functools

import jax
import jax.numpy as jnp
from jax import lax
from jax.experimental import pallas as pl
from jax.experimental.pallas import tpu as pltpu
from jax.sharding import PartitionSpec as P

STEPS = 2
MESH = pl.DeviceIdType.MESH
ANY = pl.ANY
LANES = 128
SIXTH = 1.0 / 6.0


def split_parts(v):
    high = v.astype(jnp.bfloat16)
    low = (v - high.astype(jnp.float32)).astype(jnp.bfloat16)
    return high, low


def kernel(
    groups,
    tiles,
    levels,
    wide,
    long,
    cap,
    per,
    chk_in,
    adj_in,
    cx_in,
    cy_in,
    mix_in,
    col_in,
    count_in,
    step_in,
    value_in,
    weight_in,
    kern_in,
    out,
    own,
    landed,
    adj,
    cxl,
    cy,
    mix,
    stage,
    cx,
    t0,
    t1,
    b1,
    b0,
    force,
    parts,
    onehot,
    kern,
    small,
    pack,
    misfit,
    made,
    load_sem,
    send_sem,
    recv_sem,
    snd_send,
    snd_recv,
):
    total = groups * tiles
    g = lax.axis_index("group")
    t = lax.axis_index("tile")
    me = g * tiles + t
    chunks = tiles // per
    width = per * cap

    def flat(offset):
        f = lax.rem(me + offset + total, total)
        return (lax.div(f, tiles), lax.rem(f, tiles))

    def partner(k):
        return (g, lax.rem(t + k, tiles))

    bands = long // LANES
    loads = []
    for k, (src, dst) in enumerate(
        ((chk_in, own), (cx_in, cxl), (cy_in, cy), (mix_in, mix), (adj_in, adj))
    ):
        rows = src.shape[0]
        loads.append(
            [
                pltpu.make_async_copy(
                    src.at[:, pl.ds(j * LANES, LANES)],
                    dst.at[j, pl.ds(0, rows)],
                    load_sem.at[k, j],
                )
                for j in range(bands)
            ]
        )
        for c in loads[-1]:
            c.start()

    def await_all(copies):
        for c in copies:
            c.wait()

    barrier = pltpu.get_barrier_semaphore()
    roles = [flat(o) for o in (1, -1, tiles, tiles + 1, tiles - 1, -tiles, -tiles - 1, 1 - tiles)]
    roles += [partner(k) for k in range(1, tiles)]
    for role in roles:
        pl.semaphore_signal(barrier, inc=1, device_id=role, device_id_type=MESH)

    place = lax.broadcasted_iota(jnp.int32, (1, cap), 1)
    for k in range(tiles):
        pack[k, 0:1, :] = value_in[k : k + 1, :]
        pack[k, 1:2, :] = jnp.where(place < count_in[0, k], weight_in[k : k + 1, :], 0.0)
        pack[k, 2:3, :] = col_in[k : k + 1, :].astype(jnp.float32)
        pack[k, 3:4, :] = step_in[k : k + 1, :].astype(jnp.float32)
    mix[:, pl.ds((levels - 1) * wide, wide), :] = jnp.zeros((bands, wide, LANES), jnp.float32)

    def column(ref, x):
        return jnp.concatenate(
            [ref[j, pl.ds(x, levels, stride=wide), :] for j in range(bands)], axis=1
        )

    pl.semaphore_wait(barrier, len(roles))

    def send(src, dst, k, to):
        c = pltpu.make_async_remote_copy(
            src_ref=src,
            dst_ref=dst,
            send_sem=send_sem.at[k],
            recv_sem=recv_sem.at[k],
            device_id=to,
            device_id_type=MESH,
        )
        c.start()
        return c

    main = [
        send(chk_in.at[:, pl.ds(j * LANES, LANES)], landed.at[j], 11 + j, flat(tiles))
        for j in range(bands)
    ]

    snd = []
    for k in range(1, tiles):
        to = partner(k)
        for j, (src, dst) in enumerate(
            ((kern_in.at[to[1]], kern.at[k]), (pack.at[to[1]], small.at[k]))
        ):
            c = pltpu.make_async_remote_copy(
                src_ref=src,
                dst_ref=dst,
                send_sem=snd_send.at[j, k],
                recv_sem=snd_recv.at[j, k],
                device_id=to,
                device_id_type=MESH,
            )
            c.start()
            snd.append(c)
    for j, (src, dst) in enumerate(((kern_in.at[t], kern.at[0]), (pack.at[t], small.at[0]))):
        c = pltpu.make_async_copy(src, dst, snd_recv.at[j, 0])
        c.start()
        snd.append(c)

    await_all(loads[0])
    stage[0] = column(own, wide - 2)
    stage[1] = column(own, wide - 1)
    stage[2] = column(own, 0)
    rim_low = send(stage.at[pl.ds(0, 2)], t0.at[pl.ds(0, 2)], 1, flat(tiles + 1))
    rim_high = send(stage.at[pl.ds(2, 1)], t0.at[pl.ds(wide + 2, 1)], 2, flat(tiles - 1))
    await_all(loads[1])

    def turn(x, _):
        cx[x + 1] = column(cxl, x) * SIXTH
        return 0

    lax.fori_loop(0, wide, turn, 0)
    wind_low = send(cx.at[pl.ds(wide, 1)], cx.at[pl.ds(0, 1)], 3, flat(1))
    wind_high = send(cx.at[pl.ds(1, 1)], cx.at[pl.ds(wide + 1, 1)], 4, flat(-1))

    for c in snd:
        c.wait()

    def row_of(c, r):
        return jnp.concatenate([small[c * per + k, r : r + 1, :] for k in range(per)], axis=1)

    def kern_of(c):
        return jnp.concatenate([kern[c * per + k] for k in range(per)], axis=1)

    def cell_of(c):
        cell = row_of(c, 2).astype(jnp.int32)
        cx_of = jnp.zeros_like(cell)
        for x in range(1, wide):
            cx_of = cx_of + jnp.where(cell >= x * long, 1, 0)
        return cx_of, cell - cx_of * long

    def mark(c, _):
        _, cy_of = cell_of(c)
        rows = 128
        for first in range(0, long, rows):
            at = lax.broadcasted_iota(jnp.int32, (rows, width), 0) + first
            onehot[c, first : first + rows, :] = jnp.where(at == cy_of, 1.0, 0.0).astype(
                jnp.bfloat16
            )
        return 0

    lax.fori_loop(0, chunks, mark, 0)

    def mixed(v, m):
        f = m * (pltpu.roll(v, levels - 1, 0) - v)
        return v + f - pltpu.roll(f, 1, 0)

    def along_y(v, c):
        f = (c * SIXTH) * (2.0 * pltpu.roll(v, long - 1, 1) + 5.0 * v - pltpu.roll(v, 1, 1))
        return v + pltpu.roll(f, 1, 1) - f

    def back_y(a, c):
        q = (c * SIXTH) * (pltpu.roll(a, long - 1, 1) - a)
        return a + 2.0 * pltpu.roll(q, 1, 1) + 5.0 * q - pltpu.roll(q, long - 1, 1)

    def forward(src, dst):
        def row(x, _):
            before = cx[x] * (2.0 * src[x + 2] + 5.0 * src[x + 1] - src[x])
            after = cx[x + 1] * (2.0 * src[x + 3] + 5.0 * src[x + 2] - src[x + 1])
            v = src[x + 2] + before - after
            v = mixed(along_y(v, column(cy, x)), column(mix, x))
            if dst is not None:
                dst[x + 2] = v
            high, low = split_parts(v)
            at = pl.multiple_of(x * 2 * levels, 2 * levels)
            parts[pl.ds(at, levels), :] = high
            parts[pl.ds(at + levels, levels), :] = low
            return 0

        return row

    def observe(moment):
        def one(c, _):
            picked = jnp.dot(parts[...], onehot[c], preferred_element_type=jnp.float32)
            cx_of, _ = cell_of(c)
            seen = jnp.zeros((2 * levels, width), jnp.float32)
            for x in range(wide):
                seen = seen + jnp.where(
                    cx_of == x, picked[x * 2 * levels : (x + 1) * 2 * levels], 0.0
                )
            seen = seen[:levels] + seen[levels:]
            seen = jnp.sum(seen * kern_of(c), axis=0, keepdims=True)
            gap = row_of(c, 1) * (seen - row_of(c, 0))
            misfit[c, moment : moment + 1, :] = jnp.where(
                row_of(c, 3).astype(jnp.int32) == moment, gap, 0.0
            )
            return 0

        lax.fori_loop(0, chunks, one, 0)

    def spread(moment):
        force[...] = jnp.zeros_like(force)

        def one(c, _):
            high, low = split_parts(kern_of(c) * misfit[c, moment : moment + 1, :])
            high, low = high.astype(jnp.float32), low.astype(jnp.float32)
            cx_of, _ = cell_of(c)
            rows = []
            for part in (high, low):
                for x in range(wide):
                    rows.append(jnp.where(cx_of == x, part, 0.0).astype(jnp.bfloat16))
            sums = lax.dot_general(
                jnp.concatenate(rows, axis=0),
                onehot[c],
                (((1,), (1,)), ((), ())),
                preferred_element_type=jnp.float32,
            )
            half = wide * levels
            force[...] += sums[:half] + sums[half:]
            return 0

        lax.fori_loop(0, chunks, one, 0)

    def force_at(x):
        return force[pl.ds(pl.multiple_of(x * levels, levels), levels), :]

    await_all(main)

    def place_row(x, _):
        t0[x + 2] = column(landed, x)
        return 0

    lax.fori_loop(0, wide, place_row, 0)
    await_all(loads[2])
    await_all(loads[3])
    for c in (rim_low, rim_high, wind_low, wind_high):
        c.wait()
    row = forward(t0, t1)
    for x in (0, wide - 2, wide - 1):
        row(x, 0)
    low1 = send(t1.at[pl.ds(wide, 2)], t1.at[pl.ds(0, 2)], 5, flat(1))
    high1 = send(t1.at[pl.ds(2, 1)], t1.at[pl.ds(wide + 2, 1)], 6, flat(-1))
    lax.fori_loop(1, wide - 2, row, 0)
    observe(0)
    low1.wait()
    high1.wait()
    lax.fori_loop(0, wide, forward(t1, None), 0)
    observe(1)

    await_all(loads[4])
    spread(1)

    def first_back(x, _):
        a = mixed(column(adj, x) + force_at(x), column(mix, x))
        b1[x + 2] = back_y(a, column(cy, x))
        return 0

    def back_x(src, x):
        d0 = src[x + 2]
        d1 = src[x + 3]
        q_before = cx[x] * (d0 - src[x + 1])
        q_here = cx[x + 1] * (d1 - d0)
        q_after = cx[x + 2] * (src[x + 4] - d1)
        return d0 + 2.0 * q_before + 5.0 * q_here - q_after

    def rims_back(buf, k):
        return (
            send(buf.at[pl.ds(wide + 1, 1)], buf.at[pl.ds(1, 1)], k, flat(1)),
            send(buf.at[pl.ds(2, 2)], buf.at[pl.ds(wide + 2, 2)], k + 1, flat(-1)),
        )

    for x in (0, 1, wide - 1):
        first_back(x, 0)
    rims = rims_back(b1, 7)
    lax.fori_loop(2, wide - 1, first_back, 0)
    spread(0)
    for c in rims:
        c.wait()

    def second_back(x, _):
        a = mixed(back_x(b1, x) + force_at(x), column(mix, x))
        b0[x + 2] = back_y(a, column(cy, x))
        return 0

    for x in (0, 1, wide - 1):
        second_back(x, 0)
    rims = rims_back(b0, 9)
    lax.fori_loop(2, wide - 1, second_back, 0)

    def last(x, _):
        v = back_x(b0, x)
        for j in range(bands):
            made[j, pl.ds(x, levels, stride=wide), :] = v[:, j * LANES : (j + 1) * LANES]
        return 0

    lax.fori_loop(1, wide - 2, last, 0)
    for c in rims:
        c.wait()
    for x in (0, wide - 2, wide - 1):
        last(x, 0)
    stores = [
        pltpu.make_async_copy(
            made.at[j], out.at[:, pl.ds(j * LANES, LANES)], load_sem.at[5, j]
        )
        for j in range(bands)
    ]
    for c in stores:
        c.start()
    await_all(stores)


def on_device(
    groups,
    tiles,
    checkpoint,
    adjoint_in,
    courant_x,
    courant_y,
    mixing,
    snd_column,
    snd_count,
    snd_step,
    snd_value,
    snd_weight,
    snd_kernel,
):
    levels, wide, long = checkpoint.shape
    cap = snd_column.shape[2]
    per = 2 if tiles % 2 == 0 else 1
    f32 = jnp.float32
    plane = (levels * wide, long)
    bands = long // LANES
    banded = (bands, levels * wide, LANES)
    rimmed = (wide + 4, levels, long)
    vmem = pl.BlockSpec(memory_space=pltpu.VMEM)
    smem = pl.BlockSpec(memory_space=pltpu.SMEM)
    anywhere = pl.BlockSpec(memory_space=ANY)
    result = pl.pallas_call(
        functools.partial(kernel, groups, tiles, levels, wide, long, cap, per),
        out_shape=jax.ShapeDtypeStruct(plane, f32),
        in_specs=[anywhere] * 5 + [vmem, smem, vmem, vmem, vmem, anywhere],
        out_specs=anywhere,
        scratch_shapes=[
            pltpu.VMEM(banded, f32),
            pltpu.VMEM(banded, f32),
            pltpu.VMEM(banded, f32),
            pltpu.VMEM(banded, f32),
            pltpu.VMEM(banded, f32),
            pltpu.VMEM(banded, f32),
            pltpu.VMEM((3, levels, long), f32),
            pltpu.VMEM((wide + 2, levels, long), f32),
            pltpu.VMEM(rimmed, f32),
            pltpu.VMEM(rimmed, f32),
            pltpu.VMEM(rimmed, f32),
            pltpu.VMEM(rimmed, f32),
            pltpu.VMEM(plane, f32),
            pltpu.VMEM((2 * levels * wide, long), jnp.bfloat16),
            pltpu.VMEM((tiles // per, long, per * cap), jnp.bfloat16),
            pltpu.VMEM((tiles, levels, cap), f32),
            pltpu.VMEM((tiles, 8, cap), f32),
            pltpu.VMEM((tiles, 8, cap), f32),
            pltpu.VMEM((tiles // per, 8, per * cap), f32),
            pltpu.VMEM(banded, f32),
            pltpu.SemaphoreType.DMA((6, bands)),
            pltpu.SemaphoreType.DMA((11 + bands,)),
            pltpu.SemaphoreType.DMA((11 + bands,)),
            pltpu.SemaphoreType.DMA((2, tiles)),
            pltpu.SemaphoreType.DMA((2, tiles)),
        ],
        compiler_params=pltpu.CompilerParams(
            collective_id=0, has_side_effects=True, vmem_limit_bytes=48 * 1024 * 1024
        ),
        name="window",
    )(
        checkpoint.reshape(plane),
        adjoint_in.reshape(plane),
        courant_x.reshape(plane),
        courant_y.reshape(plane),
        mixing.reshape(-1, long),
        snd_column.reshape(tiles, cap),
        snd_count,
        snd_step.reshape(tiles, cap),
        snd_value.reshape(tiles, cap),
        snd_weight.reshape(tiles, cap),
        snd_kernel.reshape(tiles, levels, cap),
    )
    return result.reshape(checkpoint.shape)


def solution(mesh):
    return jax.shard_map(
        functools.partial(on_device, mesh.shape["group"], mesh.shape["tile"]),
        mesh=mesh,
        in_specs=(
            P(None, ("group", "tile"), None),
            P(None, ("group", "tile"), None),
            P(None, ("group", "tile"), None),
            P(None, ("group", "tile"), None),
            P(None, ("group", "tile"), None),
            P(("group", "tile"), None, None),
            P(("group", "tile"), None),
            P(("group", "tile"), None, None),
            P(("group", "tile"), None, None),
            P(("group", "tile"), None, None),
            P(("group", "tile"), None, None, None),
        ),
        out_specs=P(None, ("group", "tile"), None),
        check_vma=False,
    )
```

time: 145 us -> 51.8 us (0.36)
  starting transfers between devices: 45.2 us -> 0 us
  Pallas kernels: 0 us -> 43.3 us
  other arithmetic: 37.4 us -> 0 us
  local copies, waits for them, and re-layouts: 41.3 us -> 8.1 us
  waiting for transfers between devices: 20.1 us -> 0 us
    pallas_call x0 -> x1, Pallas kernels: none -> 43.3 us  [on_device(): pl.pallas_call(functools.partial(kernel, groups, tiles, levels, wide, lon...]
    all_to_all x5 -> x0, starting transfers between devices: 25 us -> none  [the longest x1 7.41 us: on_device(): lax.all_to_all(snd_column, 'tile', split_axis=1, concat_axis=0, tiled=True)]
    ppermute x11 -> x0, starting transfers between devices: 20.2 us -> none  [the longest x5 12.6 us: with_halo(): lax.ppermute(lax.slice_in_dim(block, 0, width, axis=dim), axis, backward)]
    scatter-add x2 -> x0, other arithmetic: 18.4 us -> none  [on_device(): jnp.zeros((levels, width_x * width_y), jnp.float32).at[:, cell_index]]
    gather x2 -> x0, local copies, waits for them, and re-layouts: 13.6 us -> none  [on_device(): jnp.take(flattened, cell_index, axis=1)]
    reshape x5 -> x0, local copies, waits for them, and re-layouts: 11 us -> none  [the longest x2 9.79 us: on_device(): forcings.append(forcing.reshape(levels, width_x, width_y))]
    ppermute x11 -> x0, waiting for transfers between devices: 10.3 us -> none  [the longest x5 7 us: with_halo(): lax.ppermute(lax.slice_in_dim(block, block.shape[dim] - width, None, axis...]
    all_to_all x5 -> x0, waiting for transfers between devices: 9.83 us -> none  [the longest x1 6.32 us: on_device(): lax.all_to_all(snd_step, 'tile', split_axis=1, concat_axis=0, tiled=True)]
  transfers between devices with their start and end apart: 16 -> 0, of which waited for: 7 -> 0; matrix products, arithmetic and copies ran while one was open for 38% -> 0% of each run, Pallas kernels for 0% -> 0%
where the time goes in v1:
time: 51.8 us; the launch traced here: 51.4 us
  Pallas kernels  43.3 us (84%)
  local copies, waits for them, and re-layouts  8.1 us (16%)
    pallas_call x1, Pallas kernels, on_device(): pl.pallas_call(functools.partial(kernel, groups, tiles, levels, wide, lon...  43.3 us
    unnamed x23, local copies, waits for them, and re-layouts  8.1 us

profile of v1, /device:TPU:0, one launch (start us, length us, event | category | flops | bytes accessed | tf_op | source)
XLA Modules:
  0.0 51.4 jit_solution(10289482632812478793)
XLA Ops:
  0.0 0.0 copy-start.9
  0.0 0.0 copy-start.8
  0.0 0.0 copy-start.7
  0.0 0.0 copy-start.6
  0.0 0.0 copy-start.10
  0.0 0.7 %copy-done.9 = f32[1,8,128]{2,1,0:T(8,128)S(1)} copy-done((f32[1,8,128]{2,1,0:T(8,128)S(1)}, f32[1,8,128]{2,1,0:T(8,128)}, u32[]{:S(2)}) %copy-start.9) | copy-done | bytes 4120
  0.7 0.0 copy-done.8
  0.7 0.0 copy-done.7
  0.7 0.0 copy-done.6
  0.7 0.0 copy-done.10
  0.7 0.0 copy-start
  0.7 1.1 %copy-done = f32[16,16,768]{2,1,0:T(8,128)S(1)} copy-done((f32[16,16,768]{2,1,0:T(8,128)S(1)}, f32[16,16,768]{2,1,0:T(8,128)}, u32[]{:S(2)}) %copy-start) | copy-done | bytes 786456
  1.9 0.0 copy-start.1
  1.9 1.1 %copy-done.1 = f32[16,16,768]{2,1,0:T(8,128)S(1)} copy-done((f32[16,16,768]{2,1,0:T(8,128)S(1)}, f32[16,16,768]{2,1,0:T(8,128)}, u32[]{:S(2)}) %copy-start.1) | copy-done | bytes 786456
  3.0 0.0 copy-start.2
  3.0 1.1 %copy-done.2 = f32[16,16,768]{2,1,0:T(8,128)S(1)} copy-done((f32[16,16,768]{2,1,0:T(8,128)S(1)}, f32[16,16,768]{2,1,0:T(8,128)}, u32[]{:S(2)}) %copy-start.2) | copy-done | bytes 786456
  4.1 0.0 copy-start.3
  4.1 1.1 %copy-done.3 = f32[16,16,768]{2,1,0:T(8,128)S(1)} copy-done((f32[16,16,768]{2,1,0:T(8,128)S(1)}, f32[16,16,768]{2,1,0:T(8,128)}, u32[]{:S(2)}) %copy-start.3) | copy-done | bytes 786456
  5.3 0.0 copy-start.4
  5.3 1.1 %copy-done.4 = f32[15,16,768]{2,1,0:T(8,128)S(1)} copy-done((f32[15,16,768]{2,1,0:T(8,128)S(1)}, f32[15,16,768]{2,1,0:T(8,128)}, u32[]{:S(2)}) %copy-start.4) | copy-done | bytes 737304
  6.4 0.0 copy-start.5
  6.4 0.8 %copy-done.5 = f32[1,8,16,128]{3,2,1,0:T(8,128)S(1)} copy-done((f32[1,8,16,128]{3,2,1,0:T(8,128)S(1)}, f32[1,8,16,128]{3,2,1,0:T(8,128)}, u32[]{:S(2)}) %copy-start.5) | copy-done | bytes 65560
  7.2 43.3 %window.1 = f32[256,768]{1,0:T(8,128)S(1)} custom-call(f32[256,768]{1,0:T(8,128)S(1)} %bitcast.12, f32[256,768]{1,0:T(8,128)S(1)} %bitcast.13, f32[256,768]{1,0:T(8,128)S(1)} %bitcast.14, f32[256,768]{1,0:T(8,128)S(1)} %bitcast.15, f32[240,768]{1,0:T(8,128)S(1)} %bitcast.16, s32[8,128]{1,0:T(8,128)S(1)} %bitcast.18, s32[1,8]{1,0:T(1,128)S(1)} %copy-done.10, ...), custom_call_target="tpu_custom_call" | custom-call | tf_op jit(solution)/shard_map/window/pallas_call | solution.py:393
  50.6 0.9 %copy.13 = f32[16,16,768]{2,1,0:T(8,128)} copy(f32[16,16,768]{2,1,0:T(8,128)S(1)} %bitcast.11) | data formatting | bytes 1572864
Async XLA Ops:
  0.0 0.7 %copy-start.9 = (f32[1,8,128]{2,1,0:T(8,128)S(1)}, f32[1,8,128]{2,1,0:T(8,128)}, u32[]{:S(2)}) copy-start(f32[1,8,128]{2,1,0:T(8,128)} %param.20) | copy-start | bytes 12292
  0.0 0.7 %copy-start.8 = (f32[1,8,128]{2,1,0:T(8,128)S(1)}, f32[1,8,128]{2,1,0:T(8,128)}, u32[]{:S(2)}) copy-start(f32[1,8,128]{2,1,0:T(8,128)} %param.19) | copy-start | bytes 12292
  0.0 0.7 %copy-start.7 = (s32[1,8,128]{2,1,0:T(8,128)S(1)}, s32[1,8,128]{2,1,0:T(8,128)}, u32[]{:S(2)}) copy-start(s32[1,8,128]{2,1,0:T(8,128)} %param.18) | copy-start | bytes 12292
  0.0 0.7 %copy-start.6 = (s32[1,8,128]{2,1,0:T(8,128)S(1)}, s32[1,8,128]{2,1,0:T(8,128)}, u32[]{:S(2)}) copy-start(s32[1,8,128]{2,1,0:T(8,128)} %param.16) | copy-start | bytes 12292
  0.0 0.7 %copy-start.10 = (s32[1,8]{1,0:T(1,128)S(1)}, s32[1,8]{1,0:T(1,128)}, u32[]{:S(2)}) copy-start(s32[1,8]{1,0:T(1,128)} %count_in.1) | copy-start | bytes 100
  0.7 1.1 %copy-start = (f32[16,16,768]{2,1,0:T(8,128)S(1)}, f32[16,16,768]{2,1,0:T(8,128)}, u32[]{:S(2)}) copy-start(f32[16,16,768]{2,1,0:T(8,128)} %param.11) | copy-start | bytes 2359300
  1.9 1.1 %copy-start.1 = (f32[16,16,768]{2,1,0:T(8,128)S(1)}, f32[16,16,768]{2,1,0:T(8,128)}, u32[]{:S(2)}) copy-start(f32[16,16,768]{2,1,0:T(8,128)} %param.12) | copy-start | bytes 2359300
  3.0 1.1 %copy-start.2 = (f32[16,16,768]{2,1,0:T(8,128)S(1)}, f32[16,16,768]{2,1,0:T(8,128)}, u32[]{:S(2)}) copy-start(f32[16,16,768]{2,1,0:T(8,128)} %param.13) | copy-start | bytes 2359300
  4.1 1.1 %copy-start.3 = (f32[16,16,768]{2,1,0:T(8,128)S(1)}, f32[16,16,768]{2,1,0:T(8,128)}, u32[]{:S(2)}) copy-start(f32[16,16,768]{2,1,0:T(8,128)} %param.14) | copy-start | bytes 2359300
  5.3 1.1 %copy-start.4 = (f32[15,16,768]{2,1,0:T(8,128)S(1)}, f32[15,16,768]{2,1,0:T(8,128)}, u32[]{:S(2)}) copy-start(f32[15,16,768]{2,1,0:T(8,128)} %param.15) | copy-start | bytes 2211844
  6.4 0.8 %copy-start.5 = (f32[1,8,16,128]{3,2,1,0:T(8,128)S(1)}, f32[1,8,16,128]{3,2,1,0:T(8,128)}, u32[]{:S(2)}) copy-start(f32[1,8,16,128]{3,2,1,0:T(8,128)} %param.21) | copy-start | bytes 196612

commit v2 on v1

--- a/solution.py
+++ b/solution.py
@@ -9,7 +9,7 @@
 
 STEPS = 2
 MESH = pl.DeviceIdType.MESH
-ANY = pl.ANY
+ANY = pltpu.HBM
 LANES = 128
 SIXTH = 1.0 / 6.0
 
@@ -60,6 +60,12 @@
     pack,
     misfit,
     made,
+    col,
+    count,
+    step,
+    value,
+    weight,
+    light_sem,
     load_sem,
     send_sem,
     recv_sem,
@@ -80,6 +86,20 @@
     def partner(k):
         return (g, lax.rem(t + k, tiles))
 
+    light = [
+        pltpu.make_async_copy(src, dst, light_sem.at[k])
+        for k, (src, dst) in enumerate(
+            (
+                (col_in, col),
+                (count_in, count),
+                (step_in, step),
+                (value_in, value),
+                (weight_in, weight),
+            )
+        )
+    ]
+    for c in light:
+        c.start()
     bands = long // LANES
     loads = []
     for k, (src, dst) in enumerate(
@@ -109,12 +129,13 @@
     for role in roles:
         pl.semaphore_signal(barrier, inc=1, device_id=role, device_id_type=MESH)
 
+    await_all(light)
     place = lax.broadcasted_iota(jnp.int32, (1, cap), 1)
     for k in range(tiles):
-        pack[k, 0:1, :] = value_in[k : k + 1, :]
-        pack[k, 1:2, :] = jnp.where(place < count_in[0, k], weight_in[k : k + 1, :], 0.0)
-        pack[k, 2:3, :] = col_in[k : k + 1, :].astype(jnp.float32)
-        pack[k, 3:4, :] = step_in[k : k + 1, :].astype(jnp.float32)
+        pack[k, 0:1, :] = value[k : k + 1, :]
+        pack[k, 1:2, :] = jnp.where(place < count[0, k], weight[k : k + 1, :], 0.0)
+        pack[k, 2:3, :] = col[k : k + 1, :].astype(jnp.float32)
+        pack[k, 3:4, :] = step[k : k + 1, :].astype(jnp.float32)
     mix[:, pl.ds((levels - 1) * wide, wide), :] = jnp.zeros((bands, wide, LANES), jnp.float32)
 
     def column(ref, x):
@@ -387,13 +408,11 @@
     bands = long // LANES
     banded = (bands, levels * wide, LANES)
     rimmed = (wide + 4, levels, long)
-    vmem = pl.BlockSpec(memory_space=pltpu.VMEM)
-    smem = pl.BlockSpec(memory_space=pltpu.SMEM)
     anywhere = pl.BlockSpec(memory_space=ANY)
     result = pl.pallas_call(
         functools.partial(kernel, groups, tiles, levels, wide, long, cap, per),
         out_shape=jax.ShapeDtypeStruct(plane, f32),
-        in_specs=[anywhere] * 5 + [vmem, smem, vmem, vmem, vmem, anywhere],
+        in_specs=[anywhere] * 11,
         out_specs=anywhere,
         scratch_shapes=[
             pltpu.VMEM(banded, f32),
@@ -416,6 +435,12 @@
             pltpu.VMEM((tiles, 8, cap), f32),
             pltpu.VMEM((tiles // per, 8, per * cap), f32),
             pltpu.VMEM(banded, f32),
+            pltpu.VMEM((tiles, cap), jnp.int32),
+            pltpu.SMEM((1, tiles), jnp.int32),
+            pltpu.VMEM((tiles, cap), jnp.int32),
+            pltpu.VMEM((tiles, cap), f32),
+            pltpu.VMEM((tiles, cap), f32),
+            pltpu.SemaphoreType.DMA((5,)),
             pltpu.SemaphoreType.DMA((6, bands)),
             pltpu.SemaphoreType.DMA((11 + bands,)),
             pltpu.SemaphoreType.DMA((11 + bands,)),
@@ -427,17 +452,22 @@
         ),
         name="window",
     )(
-        checkpoint.reshape(plane),
-        adjoint_in.reshape(plane),
-        courant_x.reshape(plane),
-        courant_y.reshape(plane),
-        mixing.reshape(-1, long),
-        snd_column.reshape(tiles, cap),
-        snd_count,
-        snd_step.reshape(tiles, cap),
-        snd_value.reshape(tiles, cap),
-        snd_weight.reshape(tiles, cap),
-        snd_kernel.reshape(tiles, levels, cap),
+        *(
+            pltpu.with_memory_space_constraint(v, pltpu.HBM)
+            for v in (
+                checkpoint.reshape(plane),
+                adjoint_in.reshape(plane),
+                courant_x.reshape(plane),
+                courant_y.reshape(plane),
+                mixing.reshape(-1, long),
+                snd_column.reshape(tiles, cap),
+                snd_count,
+                snd_step.reshape(tiles, cap),
+                snd_value.reshape(tiles, cap),
+                snd_weight.reshape(tiles, cap),
+                snd_kernel.reshape(tiles, levels, cap),
+            )
+        )
     )
     return result.reshape(checkpoint.shape)
 

time: 51.8 us -> 43.8 us (0.85)
  local copies, waits for them, and re-layouts: 8.1 us -> 0.88 us
  Pallas kernels: 43.3 us -> 42.7 us
    unnamed x23 -> x1, local copies, waits for them, and re-layouts: 8.1 us -> 0.88 us
    pallas_call x1, Pallas kernels: 43.3 us -> 42.7 us  [on_device(): pl.pallas_call(functools.partial(kernel, groups, tiles, levels, wide, lon...]
where the time goes in v2:
time: 43.8 us; the launch traced here: 43.6 us
  Pallas kernels  42.7 us (97%)
  local copies, waits for them, and re-layouts  0.88 us (2%)
    pallas_call x1, Pallas kernels, on_device(): pl.pallas_call(functools.partial(kernel, groups, tiles, levels, wide, lon...  42.7 us
    unnamed x1, local copies, waits for them, and re-layouts  0.88 us

profile of v2, /device:TPU:0, one launch (start us, length us, event | category | flops | bytes accessed | tf_op | source)
XLA Modules:
  0.0 43.6 jit_solution(3255410195914972161)
XLA Ops:
  0.0 42.7 %window.1 = f32[256,768]{1,0:T(8,128)S(1)} custom-call(f32[256,768]{1,0:T(8,128)} %bitcast.12, f32[256,768]{1,0:T(8,128)} %bitcast.13, f32[256,768]{1,0:T(8,128)} %bitcast.14, f32[256,768]{1,0:T(8,128)} %bitcast.15, f32[240,768]{1,0:T(8,128)} %bitcast.16, s32[8,128]{1,0:T(8,128)} %bitcast.18, s32[1,8]{1,0:T(1,128)} %count_in.1, s32[8,128]{1,0:T(8,128)} %bitcast.19, ...), custom_call_target="tpu_custom_call" | custom-call | tf_op jit(solution)/shard_map/window/pallas_call | solution.py:412
  42.7 0.9 %copy.13 = f32[16,16,768]{2,1,0:T(8,128)} copy(f32[16,16,768]{2,1,0:T(8,128)S(1)} %bitcast.11) | data formatting | bytes 1572864

commit v3 on v2

--- a/solution.py
+++ b/solution.py
@@ -11,6 +11,7 @@
 MESH = pl.DeviceIdType.MESH
 ANY = pltpu.HBM
 LANES = 128
+PER = 4
 SIXTH = 1.0 / 6.0
 
 
@@ -55,6 +56,11 @@
     force,
     parts,
     onehot,
+    cyx,
+    mixx,
+    adjx,
+    line,
+    lines,
     kern,
     small,
     pack,
@@ -195,6 +201,12 @@
         cx[x + 1] = column(cxl, x) * SIXTH
         return 0
 
+    def turn_rest(x, _):
+        cyx[x] = column(cy, x) * SIXTH
+        mixx[x] = column(mix, x)
+        adjx[x] = column(adj, x)
+        return 0
+
     lax.fori_loop(0, wide, turn, 0)
     wind_low = send(cx.at[pl.ds(wide, 1)], cx.at[pl.ds(0, 1)], 3, flat(1))
     wind_high = send(cx.at[pl.ds(1, 1)], cx.at[pl.ds(wide + 1, 1)], 4, flat(-1))
@@ -227,33 +239,68 @@
 
     lax.fori_loop(0, chunks, mark, 0)
 
+    lane = lax.broadcasted_iota(jnp.int32, (levels, LANES), 1)
+    at_first = lane == 0
+    at_last = lane == LANES - 1
+
+    def get(ref, x):
+        return [ref[x, :, j * LANES : (j + 1) * LANES] for j in range(bands)]
+
+    def put(ref, x, v):
+        for j in range(bands):
+            ref[x, :, j * LANES : (j + 1) * LANES] = v[j]
+
+    def each(f, *lists):
+        return [f(*items) for items in zip(*lists)]
+
+    def ahead(v):
+        r = [pltpu.roll(b, LANES - 1, 1) for b in v]
+        return [jnp.where(at_last, r[(j + 1) % bands], r[j]) for j in range(bands)]
+
+    def behind(v):
+        r = [pltpu.roll(b, 1, 1) for b in v]
+        return [jnp.where(at_first, r[j - 1], r[j]) for j in range(bands)]
+
     def mixed(v, m):
         f = m * (pltpu.roll(v, levels - 1, 0) - v)
         return v + f - pltpu.roll(f, 1, 0)
 
-    def along_y(v, c):
-        f = (c * SIXTH) * (2.0 * pltpu.roll(v, long - 1, 1) + 5.0 * v - pltpu.roll(v, 1, 1))
-        return v + pltpu.roll(f, 1, 1) - f
-
-    def back_y(a, c):
-        q = (c * SIXTH) * (pltpu.roll(a, long - 1, 1) - a)
-        return a + 2.0 * pltpu.roll(q, 1, 1) + 5.0 * q - pltpu.roll(q, long - 1, 1)
+    def flux(c, after, here, before):
+        return c * (2.0 * after + 5.0 * here - before)
+
+    def gather_back(a, before, here, after):
+        return a + 2.0 * before + 5.0 * here - after
 
     def forward(src, dst):
-        def row(x, _):
-            before = cx[x] * (2.0 * src[x + 2] + 5.0 * src[x + 1] - src[x])
-            after = cx[x + 1] * (2.0 * src[x + 3] + 5.0 * src[x + 2] - src[x + 1])
-            v = src[x + 2] + before - after
-            v = mixed(along_y(v, column(cy, x)), column(mix, x))
-            if dst is not None:
-                dst[x + 2] = v
-            high, low = split_parts(v)
+        def row(x, fresh):
+            if fresh:
+                lead = each(flux, get(cx, x), get(src, x + 2), get(src, x + 1), get(src, x))
+            else:
+                lead = get(line, 0)
+            here = get(src, x + 2)
+            trail = each(flux, get(cx, x + 1), get(src, x + 3), here, get(src, x + 1))
+            put(line, 0, trail)
+            v = each(lambda p, q, r: p + q - r, here, lead, trail)
+            f = each(flux, get(cyx, x), ahead(v), v, behind(v))
+            v = each(lambda p, q, r: p + q - r, v, behind(f), f)
             at = pl.multiple_of(x * 2 * levels, 2 * levels)
-            parts[pl.ds(at, levels), :] = high
-            parts[pl.ds(at + levels, levels), :] = low
+            for j, (b, m) in enumerate(zip(v, get(mixx, x))):
+                b = mixed(b, m)
+                across = slice(j * LANES, (j + 1) * LANES)
+                if dst is not None:
+                    dst[x + 2, :, across] = b
+                high, low = split_parts(b)
+                parts[pl.ds(at, levels), across] = high
+                parts[pl.ds(at + levels, levels), across] = low
+
+        return row
+
+    def run(first, last, row):
+        def body(x, _):
+            row(x, False)
             return 0
 
-        return row
+        lax.fori_loop(first, last, body, 0)
 
     def observe(moment):
         def one(c, _):
@@ -275,15 +322,13 @@
         lax.fori_loop(0, chunks, one, 0)
 
     def spread(moment):
-        force[...] = jnp.zeros_like(force)
-
-        def one(c, _):
+        def one(c, first):
             high, low = split_parts(kern_of(c) * misfit[c, moment : moment + 1, :])
             high, low = high.astype(jnp.float32), low.astype(jnp.float32)
             cx_of, _ = cell_of(c)
             rows = []
-            for part in (high, low):
-                for x in range(wide):
+            for x in range(wide):
+                for part in (high, low):
                     rows.append(jnp.where(cx_of == x, part, 0.0).astype(jnp.bfloat16))
             sums = lax.dot_general(
                 jnp.concatenate(rows, axis=0),
@@ -291,15 +336,26 @@
                 (((1,), (1,)), ((), ())),
                 preferred_element_type=jnp.float32,
             )
-            half = wide * levels
-            force[...] += sums[:half] + sums[half:]
+            for x in range(wide):
+                at = 2 * x * levels
+                v = sums[at : at + levels] + sums[at + levels : at + 2 * levels]
+                force[x] = v if first else force[x] + v
+
+        one(0, True)
+
+        def more(c, _):
+            one(c, False)
             return 0
 
-        lax.fori_loop(0, chunks, one, 0)
-
-    def force_at(x):
-        return force[pl.ds(pl.multiple_of(x * levels, levels), levels), :]
-
+        if chunks > 1:
+            lax.fori_loop(1, chunks, more, 0)
+
+    def get_force(x):
+        return get(force, x)
+
+    for k in (2, 3, 4):
+        await_all(loads[k])
+    lax.fori_loop(0, wide, turn_rest, 0)
     await_all(main)
 
     def place_row(x, _):
@@ -307,37 +363,51 @@
         return 0
 
     lax.fori_loop(0, wide, place_row, 0)
-    await_all(loads[2])
-    await_all(loads[3])
     for c in (rim_low, rim_high, wind_low, wind_high):
         c.wait()
     row = forward(t0, t1)
-    for x in (0, wide - 2, wide - 1):
-        row(x, 0)
+    row(wide - 2, True)
+    row(wide - 1, False)
+    row(0, True)
     low1 = send(t1.at[pl.ds(wide, 2)], t1.at[pl.ds(0, 2)], 5, flat(1))
     high1 = send(t1.at[pl.ds(2, 1)], t1.at[pl.ds(wide + 2, 1)], 6, flat(-1))
-    lax.fori_loop(1, wide - 2, row, 0)
+    run(1, wide - 2, row)
     observe(0)
+    row = forward(t1, None)
+    row(2, True)
+    run(3, wide - 1, row)
     low1.wait()
     high1.wait()
-    lax.fori_loop(0, wide, forward(t1, None), 0)
+    row(0, True)
+    row(1, False)
+    row(wide - 1, True)
     observe(1)
 
-    await_all(loads[4])
     spread(1)
 
-    def first_back(x, _):
-        a = mixed(column(adj, x) + force_at(x), column(mix, x))
-        b1[x + 2] = back_y(a, column(cy, x))
-        return 0
-
-    def back_x(src, x):
-        d0 = src[x + 2]
-        d1 = src[x + 3]
-        q_before = cx[x] * (d0 - src[x + 1])
-        q_here = cx[x + 1] * (d1 - d0)
-        q_after = cx[x + 2] * (src[x + 4] - d1)
-        return d0 + 2.0 * q_before + 5.0 * q_here - q_after
+    def back_yv(x, a, dst):
+        a = each(mixed, each(lambda p, q: p + q, a, get_force(x)), get(mixx, x))
+        q = each(lambda c, p, r: c * (p - r), get(cyx, x), ahead(a), a)
+        put(dst, x + 2, each(gather_back, a, behind(q), q, ahead(q)))
+
+    def first_back(x, fresh):
+        back_yv(x, get(adjx, x), b1)
+
+    def back_x(src, x, fresh):
+        here = get(src, x + 2)
+        after = get(src, x + 3)
+        diff = lambda c, p, r: c * (p - r)
+        if fresh:
+            q_before = each(diff, get(cx, x), here, get(src, x + 1))
+            q_here = each(diff, get(cx, x + 1), after, here)
+            put(lines, x, q_before)
+            put(lines, x + 1, q_here)
+        else:
+            q_before = get(lines, x)
+            q_here = get(lines, x + 1)
+        q_after = each(diff, get(cx, x + 2), get(src, x + 4), after)
+        put(lines, x + 2, q_after)
+        return each(gather_back, here, q_before, q_here, q_after)
 
     def rims_back(buf, k):
         return (
@@ -346,34 +416,34 @@
         )
 
     for x in (0, 1, wide - 1):
-        first_back(x, 0)
+        first_back(x, True)
     rims = rims_back(b1, 7)
-    lax.fori_loop(2, wide - 1, first_back, 0)
+    run(2, wide - 1, first_back)
     spread(0)
     for c in rims:
         c.wait()
 
-    def second_back(x, _):
-        a = mixed(back_x(b1, x) + force_at(x), column(mix, x))
-        b0[x + 2] = back_y(a, column(cy, x))
-        return 0
-
-    for x in (0, 1, wide - 1):
-        second_back(x, 0)
+    def second_back(x, fresh):
+        back_yv(x, back_x(b1, x, fresh), b0)
+
+    second_back(wide - 1, True)
+    second_back(0, True)
+    second_back(1, False)
     rims = rims_back(b0, 9)
-    lax.fori_loop(2, wide - 1, second_back, 0)
-
-    def last(x, _):
-        v = back_x(b0, x)
+    run(2, wide - 1, second_back)
+
+    def last(x, fresh):
+        v = back_x(b0, x, fresh)
         for j in range(bands):
-            made[j, pl.ds(x, levels, stride=wide), :] = v[:, j * LANES : (j + 1) * LANES]
-        return 0
-
-    lax.fori_loop(1, wide - 2, last, 0)
+            made[j, pl.ds(x, levels, stride=wide), :] = v[j]
+
+    last(1, True)
+    run(2, wide - 2, last)
     for c in rims:
         c.wait()
-    for x in (0, wide - 2, wide - 1):
-        last(x, 0)
+    last(0, True)
+    last(wide - 2, True)
+    last(wide - 1, False)
     stores = [
         pltpu.make_async_copy(
             made.at[j], out.at[:, pl.ds(j * LANES, LANES)], load_sem.at[5, j]
@@ -402,7 +472,7 @@
 ):
     levels, wide, long = checkpoint.shape
     cap = snd_column.shape[2]
-    per = 2 if tiles % 2 == 0 else 1
+    per = next(k for k in (PER, 2, 1) if tiles % k == 0)
     f32 = jnp.float32
     plane = (levels * wide, long)
     bands = long // LANES
@@ -427,9 +497,14 @@
             pltpu.VMEM(rimmed, f32),
             pltpu.VMEM(rimmed, f32),
             pltpu.VMEM(rimmed, f32),
-            pltpu.VMEM(plane, f32),
+            pltpu.VMEM((wide, levels, long), f32),
             pltpu.VMEM((2 * levels * wide, long), jnp.bfloat16),
             pltpu.VMEM((tiles // per, long, per * cap), jnp.bfloat16),
+            pltpu.VMEM((wide, levels, long), f32),
+            pltpu.VMEM((wide, levels, long), f32),
+            pltpu.VMEM((wide, levels, long), f32),
+            pltpu.VMEM((1, levels, long), f32),
+            pltpu.VMEM((wide + 2, levels, long), f32),
             pltpu.VMEM((tiles, levels, cap), f32),
             pltpu.VMEM((tiles, 8, cap), f32),
             pltpu.VMEM((tiles, 8, cap), f32),

time: 43.8 us -> 42.3 us (0.966)
  Pallas kernels: 42.7 us -> 41.3 us
    pallas_call x1, Pallas kernels: 42.7 us -> 41.3 us  [on_device(): pl.pallas_call(functools.partial(kernel, groups, tiles, levels, wide, lon...]
where the time goes in v3:
time: 42.3 us; the launch traced here: 42.2 us
  Pallas kernels  41.3 us (98%)
  local copies, waits for them, and re-layouts  0.88 us (2%)
    pallas_call x1, Pallas kernels, on_device(): pl.pallas_call(functools.partial(kernel, groups, tiles, levels, wide, lon...  41.3 us
    unnamed x1, local copies, waits for them, and re-layouts  0.88 us

profile of v3, /device:TPU:0, one launch (start us, length us, event | category | flops | bytes accessed | tf_op | source)
XLA Modules:
  0.0 42.2 jit_solution(11737754816507107097)
XLA Ops:
  0.0 41.3 %window.1 = f32[256,768]{1,0:T(8,128)S(1)} custom-call(f32[256,768]{1,0:T(8,128)} %bitcast.12, f32[256,768]{1,0:T(8,128)} %bitcast.13, f32[256,768]{1,0:T(8,128)} %bitcast.14, f32[256,768]{1,0:T(8,128)} %bitcast.15, f32[240,768]{1,0:T(8,128)} %bitcast.16, s32[8,128]{1,0:T(8,128)} %bitcast.18, s32[1,8]{1,0:T(1,128)} %count_in.1, s32[8,128]{1,0:T(8,128)} %bitcast.19, ...), custom_call_target="tpu_custom_call" | custom-call | tf_op jit(solution)/shard_map/window/pallas_call | solution.py:482
  41.3 0.9 %copy.13 = f32[16,16,768]{2,1,0:T(8,128)} copy(f32[16,16,768]{2,1,0:T(8,128)S(1)} %bitcast.11) | data formatting | bytes 1572864

commit v4 on v3

--- a/solution.py
+++ b/solution.py
@@ -61,6 +61,7 @@
     adjx,
     line,
     lines,
+    swept,
     kern,
     small,
     pack,
@@ -135,13 +136,6 @@
     for role in roles:
         pl.semaphore_signal(barrier, inc=1, device_id=role, device_id_type=MESH)
 
-    await_all(light)
-    place = lax.broadcasted_iota(jnp.int32, (1, cap), 1)
-    for k in range(tiles):
-        pack[k, 0:1, :] = value[k : k + 1, :]
-        pack[k, 1:2, :] = jnp.where(place < count[0, k], weight[k : k + 1, :], 0.0)
-        pack[k, 2:3, :] = col[k : k + 1, :].astype(jnp.float32)
-        pack[k, 3:4, :] = step[k : k + 1, :].astype(jnp.float32)
     mix[:, pl.ds((levels - 1) * wide, wide), :] = jnp.zeros((bands, wide, LANES), jnp.float32)
 
     def column(ref, x):
@@ -167,6 +161,14 @@
         send(chk_in.at[:, pl.ds(j * LANES, LANES)], landed.at[j], 11 + j, flat(tiles))
         for j in range(bands)
     ]
+
+    await_all(light)
+    place = lax.broadcasted_iota(jnp.int32, (1, cap), 1)
+    for k in range(tiles):
+        pack[k, 0:1, :] = value[k : k + 1, :]
+        pack[k, 1:2, :] = jnp.where(place < count[0, k], weight[k : k + 1, :], 0.0)
+        pack[k, 2:3, :] = col[k : k + 1, :].astype(jnp.float32)
+        pack[k, 3:4, :] = step[k : k + 1, :].astype(jnp.float32)
 
     snd = []
     for k in range(1, tiles):
@@ -211,9 +213,6 @@
     wind_low = send(cx.at[pl.ds(wide, 1)], cx.at[pl.ds(0, 1)], 3, flat(1))
     wind_high = send(cx.at[pl.ds(1, 1)], cx.at[pl.ds(wide + 1, 1)], 4, flat(-1))
 
-    for c in snd:
-        c.wait()
-
     def row_of(c, r):
         return jnp.concatenate([small[c * per + k, r : r + 1, :] for k in range(per)], axis=1)
 
@@ -237,8 +236,6 @@
             )
         return 0
 
-    lax.fori_loop(0, chunks, mark, 0)
-
     lane = lax.broadcasted_iota(jnp.int32, (levels, LANES), 1)
     at_first = lane == 0
     at_last = lane == LANES - 1
@@ -270,6 +267,19 @@
 
     def gather_back(a, before, here, after):
         return a + 2.0 * before + 5.0 * here - after
+
+    def along_y(x, v, dst):
+        f = each(flux, get(cyx, x), ahead(v), v, behind(v))
+        v = each(lambda p, q, r: p + q - r, v, behind(f), f)
+        at = pl.multiple_of(x * 2 * levels, 2 * levels)
+        for j, (b, m) in enumerate(zip(v, get(mixx, x))):
+            b = mixed(b, m)
+            across = slice(j * LANES, (j + 1) * LANES)
+            if dst is not None:
+                dst[x + 2, :, across] = b
+            high, low = split_parts(b)
+            parts[pl.ds(at, levels), across] = high
+            parts[pl.ds(at + levels, levels), across] = low
 
     def forward(src, dst):
         def row(x, fresh):
@@ -280,18 +290,7 @@
             here = get(src, x + 2)
             trail = each(flux, get(cx, x + 1), get(src, x + 3), here, get(src, x + 1))
             put(line, 0, trail)
-            v = each(lambda p, q, r: p + q - r, here, lead, trail)
-            f = each(flux, get(cyx, x), ahead(v), v, behind(v))
-            v = each(lambda p, q, r: p + q - r, v, behind(f), f)
-            at = pl.multiple_of(x * 2 * levels, 2 * levels)
-            for j, (b, m) in enumerate(zip(v, get(mixx, x))):
-                b = mixed(b, m)
-                across = slice(j * LANES, (j + 1) * LANES)
-                if dst is not None:
-                    dst[x + 2, :, across] = b
-                high, low = split_parts(b)
-                parts[pl.ds(at, levels), across] = high
-                parts[pl.ds(at + levels, levels), across] = low
+            along_y(x, each(lambda p, q, r: p + q - r, here, lead, trail), dst)
 
         return row
 
@@ -356,22 +355,40 @@
     for k in (2, 3, 4):
         await_all(loads[k])
     lax.fori_loop(0, wide, turn_rest, 0)
-    await_all(main)
-
-    def place_row(x, _):
-        t0[x + 2] = column(landed, x)
-        return 0
-
-    lax.fori_loop(0, wide, place_row, 0)
-    for c in (rim_low, rim_high, wind_low, wind_high):
+
+    await_all(snd)
+    lax.fori_loop(0, chunks, mark, 0)
+    for c in (wind_low, wind_high):
         c.wait()
-    row = forward(t0, t1)
-    row(wide - 2, True)
-    row(wide - 1, False)
-    row(0, True)
+
+    def sweep_x(x, across):
+        lead = flux(cx[x, :, across], t0[x + 2, :, across], t0[x + 1, :, across], t0[x, :, across])
+        here = t0[x + 2, :, across]
+        trail = flux(cx[x + 1, :, across], t0[x + 3, :, across], here, t0[x + 1, :, across])
+        swept[x, :, across] = here + lead - trail
+
+    for j in range(bands):
+        across = slice(j * LANES, (j + 1) * LANES)
+        main[j].wait()
+        for x in range(wide):
+            t0[x + 2, :, across] = landed[j, pl.ds(x, levels, stride=wide), :]
+        for x in range(2, wide - 1):
+            sweep_x(x, across)
+    rim_low.wait()
+    rim_high.wait()
+    for x in (0, 1, wide - 1):
+        for j in range(bands):
+            sweep_x(x, slice(j * LANES, (j + 1) * LANES))
+
+    def first_forward(x, fresh):
+        along_y(x, get(swept, x), t1)
+
+    first_forward(wide - 2, False)
+    first_forward(wide - 1, False)
+    first_forward(0, False)
     low1 = send(t1.at[pl.ds(wide, 2)], t1.at[pl.ds(0, 2)], 5, flat(1))
     high1 = send(t1.at[pl.ds(2, 1)], t1.at[pl.ds(wide + 2, 1)], 6, flat(-1))
-    run(1, wide - 2, row)
+    run(1, wide - 2, first_forward)
     observe(0)
     row = forward(t1, None)
     row(2, True)
@@ -505,6 +522,7 @@
             pltpu.VMEM((wide, levels, long), f32),
             pltpu.VMEM((1, levels, long), f32),
             pltpu.VMEM((wide + 2, levels, long), f32),
+            pltpu.VMEM((wide, levels, long), f32),
             pltpu.VMEM((tiles, levels, cap), f32),
             pltpu.VMEM((tiles, 8, cap), f32),
             pltpu.VMEM((tiles, 8, cap), f32),

time: 42.3 us -> 43.3 us (1.024)
  Pallas kernels: 41.3 us -> 42.2 us
    pallas_call x1, Pallas kernels: 41.3 us -> 42.2 us  [on_device(): pl.pallas_call(functools.partial(kernel, groups, tiles, levels, wide, lon...]
where the time goes in v4:
time: 43.3 us; the launch traced here: 43.1 us
  Pallas kernels  42.2 us (97%)
  local copies, waits for them, and re-layouts  0.88 us (2%)
    pallas_call x1, Pallas kernels, on_device(): pl.pallas_call(functools.partial(kernel, groups, tiles, levels, wide, lon...  42.2 us
    unnamed x1, local copies, waits for them, and re-layouts  0.88 us

profile of v4, /device:TPU:0, one launch (start us, length us, event | category | flops | bytes accessed | tf_op | source)
XLA Modules:
  0.0 43.1 jit_solution(5396645332293701542)
XLA Ops:
  0.0 42.2 %window.1 = f32[256,768]{1,0:T(8,128)S(1)} custom-call(f32[256,768]{1,0:T(8,128)} %bitcast.12, f32[256,768]{1,0:T(8,128)} %bitcast.13, f32[256,768]{1,0:T(8,128)} %bitcast.14, f32[256,768]{1,0:T(8,128)} %bitcast.15, f32[240,768]{1,0:T(8,128)} %bitcast.16, s32[8,128]{1,0:T(8,128)} %bitcast.18, s32[1,8]{1,0:T(1,128)} %count_in.1, s32[8,128]{1,0:T(8,128)} %bitcast.19, ...), custom_call_target="tpu_custom_call" | custom-call | tf_op jit(solution)/shard_map/window/pallas_call | solution.py:499
  42.2 0.9 %copy.13 = f32[16,16,768]{2,1,0:T(8,128)} copy(f32[16,16,768]{2,1,0:T(8,128)S(1)} %bitcast.11) | data formatting | bytes 1572864
